TPU v7x, 32 devices: a whole 2x2x4 slice. The times are simulated.
32 devices in a mesh: lines: 4 (over y, x), buses: 8 (over z, core).
Axes of the slice: x: 2, y: 2, z: 4, core: 2. Of those that a mesh axis runs over, the one named last changes fastest.
Arguments:
- ptdf: bfloat16 [4096, 10240], P('lines', 'buses'), may hold values from -0.078125 to 0.078125
- load: float32 [384, 10240], P(None, 'buses'), may hold values from 0.03 to 3.8, as said below
- ratings: float32 [32768], replicated, may hold values from 0.3 to 3
- line_index: int32 [4096], P('lines'), may hold values from 0 to 32767
- gen_bus: int32 [2048], P('buses'), may hold values from 0 to 10239, as said below
- gen_quad: float32 [2048], P('buses'), may hold values from 0.05 to 0.5
- gen_lin: float32 [2048], P('buses'), may hold values from 0.5 to 2.5
- gen_max: float32 [2048], P('buses'), may hold values from 0.8 to 4
- gen_start: float32 [384, 2048], P(None, 'buses'), may hold values from 0 to 2
- stor_bus: int32 [1024], P('buses'), may hold values from 0 to 1279
- stor_quad: float32 [1024], P('buses'), may hold values from 0.05 to 0.5
- stor_rate: float32 [1024], P('buses'), may hold values from 0.3 to 1.5
- stor_energy: float32 [1024], P('buses'), may hold values from 1 to 8
- stor_start: float32 [384, 1024], P(None, 'buses'), may hold values from -0.5 to 0.5
- lam_start: float32 [384], replicated, may hold values from -4 to 4
- mu_start: float32 [384, 4096], P(None, ('lines', 'buses')), may hold values from -3 to 3
- omega_start: float32 [384, 1024], P(None, 'buses'), may hold values from -2 to 2
Outputs:
- gen_out: float32 [384, 2048], P(None, 'buses')
- stor_out: float32 [384, 1024], P(None, 'buses')
- lam_out: float32 [384], replicated
- mu_out: float32 [384, 4096], P(None, ('lines', 'buses'))
- omega_out: float32 [384, 1024], P(None, 'buses')
Inputs may be any that keep to these rules, and one draw needn't show every extreme that they name: `gen_bus`: of the 256 generators of one area at most 32 sit on the buses of any one area (1280 consecutive buses); in every draw one area holds exactly 32 generators of every area, and the others of an area spread over the remaining areas as evenly as counts allow. `load`: loads are positive.
All inputs are finite; a program needn't handle non-finite values.
Results may differ from a plain program's by a relative error of at most 0.0075.
Values may be sent and summed in bfloat16 or wider, within the bound.
A program may use at most 64 MiB of HBM per device.

v0:
```python
import jax
import jax.numpy as jnp
from jax import lax
from jax.sharding import PartitionSpec as P

HOURS = 24
TAU = 0.25
SIGMA_FLOW = 4.0
SIGMA_STORE = 0.25
KAPPA = 1.0
THETA = 0.5


def reverse_cum(values, hour_count):
    total_rows, columns = values.shape
    shaped = values.reshape(total_rows // hour_count, hour_count, columns)
    summed = jnp.flip(jnp.cumsum(jnp.flip(shaped, 1), axis=1), 1)
    return summed.reshape(total_rows, columns)


def forward_cum(values, hour_count):
    total_rows, columns = values.shape
    shaped = values.reshape(total_rows // hour_count, hour_count, columns)
    return jnp.cumsum(shaped, axis=1).reshape(total_rows, columns)


def dual_step(dual_now, image_term, step_size, low_bound, high_bound):
    shifted = dual_now + step_size * image_term
    return shifted - step_size * jnp.clip(shifted / step_size, low_bound, high_bound)


def shards(
    ptdf,
    load,
    ratings,
    line_index,
    gen_bus,
    gen_quad,
    gen_lin,
    gen_max,
    gen_start,
    stor_bus,
    stor_quad,
    stor_rate,
    stor_energy,
    stor_start,
    lam_start,
    mu_start,
    omega_start,
):
    row_count = load.shape[0]
    line_count, bus_count = ptdf.shape
    gen_count = gen_bus.shape[0]
    stor_count = stor_bus.shape[0]
    device_count = lax.axis_size("buses")
    slot_count = max(8, (gen_count + device_count - 1) // device_count)
    slot_width = device_count * slot_count
    share_len = line_count // device_count
    share_start = lax.axis_index("buses") * share_len
    target = gen_bus // bus_count
    local_bus = gen_bus % bus_count
    target_hit = (target[:, None] == jnp.arange(device_count, dtype=jnp.int32)[None, :]).astype(
        jnp.int32
    )
    rank_in = jnp.sum(target_hit * jnp.cumsum(target_hit, axis=0), axis=1) - 1
    column = target * slot_count + rank_in
    slot_ids = jnp.full((slot_width,), -1, jnp.int32).at[column].set(local_bus)
    arrived = lax.all_to_all(slot_ids[None, :], "buses", split_axis=1, concat_axis=1, tiled=True)
    arrived_bus = jnp.maximum(arrived[0], 0)
    limit_block = jnp.take(ratings, line_index)
    limit_share = lax.dynamic_slice_in_dim(limit_block, share_start, share_len)
    hour_of = jnp.arange(row_count, dtype=jnp.int32) % HOURS
    last_hour = (hour_of == HOURS - 1)[:, None]
    half_energy = (0.5 * stor_energy)[None, :]
    low_bound = jnp.where(last_hour, jnp.zeros_like(half_energy), -half_energy)
    high_bound = jnp.where(last_hour, jnp.zeros_like(half_energy), half_energy)
    load_total = jnp.sum(load, axis=1)
    total_units = (gen_count + stor_count) * device_count
    dual_flow = mu_start
    gen_now, stor_now = (gen_start, stor_start)
    gen_old, stor_old = (gen_start, stor_start)
    price_level, dual_store = (lam_start, omega_start)
    for iteration in range(2):
        if iteration == 0:
            gen_mid, stor_mid = (gen_now, stor_now)
        else:
            gen_mid = gen_now + THETA * (gen_now - gen_old)
            stor_mid = stor_now + THETA * (stor_now - stor_old)
        dual_low = lax.all_gather(dual_flow.astype(jnp.bfloat16), "buses", axis=1, tiled=True)
        partial_value = jnp.dot(dual_low, ptdf, preferred_element_type=jnp.float32)
        bus_price = lax.psum(partial_value.astype(jnp.bfloat16), "lines").astype(jnp.float32)
        gen_part = jnp.take(
            lax.all_to_all(
                jnp.take(bus_price, arrived_bus, axis=1).astype(jnp.bfloat16),
                "buses",
                split_axis=1,
                concat_axis=1,
                tiled=True,
            ).astype(jnp.float32),
            column,
            axis=1,
        )
        stor_price = jnp.take(bus_price, stor_bus, axis=1)
        gen_grad = 2.0 * gen_quad * gen_mid + gen_lin + price_level[:, None] + gen_part
        gen_next = jnp.clip(gen_mid - TAU * gen_grad, 0.0, gen_max)
        stor_grad = (
            2.0 * stor_quad * stor_mid
            + price_level[:, None]
            + stor_price
            + reverse_cum(dual_store, HOURS)
        )
        stor_next = jnp.clip(stor_mid - TAU * stor_grad, -stor_rate, stor_rate)
        gen_bar = 2.0 * gen_next - gen_now
        stor_bar = 2.0 * stor_next - stor_now
        balance_term = jnp.sum(gen_bar, axis=1) + jnp.sum(stor_bar, axis=1) - load_total
        stor_inject = jnp.zeros((row_count, bus_count), jnp.float32).at[:, stor_bus].add(stor_bar)
        slotted = jnp.zeros((gen_bar.shape[0], slot_width), jnp.float32).at[:, column].set(gen_bar)
        received = lax.all_to_all(
            slotted.astype(jnp.bfloat16), "buses", split_axis=1, concat_axis=1, tiled=True
        ).astype(slotted.dtype)
        empty = jnp.zeros((received.shape[0], bus_count), jnp.float32)
        injection = empty.at[:, arrived_bus].add(received) + stor_inject - load
        inj_low = injection.astype(jnp.bfloat16)
        flow_share = lax.psum_scatter(
            lax.dot_general(
                ptdf, inj_low, (((1,), (1,)), ((), ())), preferred_element_type=jnp.float32
            ),
            "buses",
            scatter_dimension=0,
            tiled=True,
        ).T
        balance = lax.psum(balance_term, "buses")
        dual_flow = dual_step(dual_flow, flow_share, SIGMA_FLOW, -limit_share, limit_share)
        price_level = price_level + KAPPA / total_units * balance
        dual_store = dual_step(
            dual_store, forward_cum(stor_bar, HOURS), SIGMA_STORE, low_bound, high_bound
        )
        gen_old, stor_old = (gen_now, stor_now)
        gen_now, stor_now = (gen_next, stor_next)
    return (gen_now, stor_now, price_level, dual_flow, dual_store)


def solution(mesh):
    return jax.shard_map(
        shards,
        mesh=mesh,
        in_specs=(
            P("lines", "buses"),
            P(None, "buses"),
            P(),
            P("lines"),
            P("buses"),
            P("buses"),
            P("buses"),
            P("buses"),
            P(None, "buses"),
            P("buses"),
            P("buses"),
            P("buses"),
            P("buses"),
            P(None, "buses"),
            P(),
            P(None, ("lines", "buses")),
            P(None, "buses"),
        ),
        out_specs=(
            P(None, "buses"),
            P(None, "buses"),
            P(),
            P(None, ("lines", "buses")),
            P(None, "buses"),
        ),
        check_vma=False,
    )
```

profile of v0, /device:TPU:0, one launch (start us, length us, event | category | flops | bytes accessed | tf_op | source)
XLA Modules:
  0.0 342.7 jit_solution(5107921957427476958)
XLA Ops:
  11.1 6.4 %all-to-all-start = ((s32[1,8,32]{2,0,1:T(1,128)}), s32[1,8,32]{2,0,1:T(1,128)S(1)}, u32[]{:S(2)}, u32[]{:S(2)}) async-start(s32[1,8,32]{2,0,1:T(1,128)} %all_to_all.30), calls=%async_computation | async-start | bytes 8192 | tf_op jit(solution)/shard_map/all_to_all | solution.py:68
  18.4 15.0 %all_gather.6 = bf16[384,1024]{1,0:T(8,128)(2,1)S(1)} all-gather(bf16[384,128]{1,0:T(8,128)(2,1)S(1)} %convert_element_type.65), channel_id=1, replica_groups=mesh['lines'=4,'buses'=8] {'buses'}, dimensions={1}, use_global_device_ids=true | all-gather | bytes 884736 | tf_op jit(solution)/shard_map/all_gather | solution.py:89
  33.4 2.2 convolution_convert_fusion.1
  37.1 50.5 %all-reduce.3.cloned.1.call-done = bf16[384,1280]{1,0:T(8,128)(2,1)} async-done(((bf16[384,1280]{1,0:T(8,128)(2,1)}), bf16[384,1280]{1,0:T(8,128)(2,1)}) %all-reduce.3.cloned.1.call-update) | async-done | bytes 983056 | tf_op jit(solution)/shard_map/psum | solution.py:91
  87.7 2.5 copy.69
  90.2 2.7 gather_fusion.1
  93.7 4.6 %all-to-all-start.1 = ((bf16[384,8,32]{0,2,1:T(8,128)(2,1)}), bf16[384,8,32]{0,2,1:T(8,128)(2,1)}, u32[]{:S(2)}, u32[]{:S(2)}) async-start(bf16[384,8,32]{0,2,1:T(8,128)(2,1)} %bitcast.4), calls=%async_computation.1 | async-start | bytes 393216 | tf_op jit(solution)/shard_map/all_to_all | solution.py:93
  100.8 2.9 copy.78
  103.8 3.0 all-to-all-done.1
  111.3 2.2 scatter_custom_fusion.1
  115.1 4.0 %all-to-all-start.2 = ((bf16[384,8,32]{0,2,1:T(8,128)(2,1)}), bf16[384,8,32]{0,2,1:T(8,128)(2,1)}, u32[]{:S(2)}, u32[]{:S(2)}) async-start(bf16[384,8,32]{0,2,1:T(8,128)(2,1)} %bitcast.136), calls=%async_computation.2 | async-start | bytes 393216 | tf_op jit(solution)/shard_map/all_to_all | solution.py:118
  119.9 3.1 gather_fusion.3
  124.7 2.5 fusion.53
  129.2 4.7 %scatter_custom_fusion.2 = f32[384,1280]{0,1:T(8,128)} fusion(s32[384]{0:T(512)} %add_reduce_fusion, f32[]{:T(128)} %constant.64.clone.1, f32[384,128]{0,1:T(8,128)S(1)} %copy.77, f32[]{:T(128)} %constant.140, f32[384,256]{0,1:T(8,128)} %bitcast_convert_fusion.4), kind=kCustom, calls=%fused_computation.22 | custom fusion | flops 294912 | bytes 2556928 | tf_op jit(solution)/shard_map/add | solution.py:122
  133.8 4.5 %convolution_bitcast_fusion.1 = f32[1024,384]{0,1:T(8,128)} fusion(bf16[1024,1280]{1,0:T(8,128)(2,1)S(1)} %copy-done, f32[384,1280]{0,1:T(8,128)} %scatter_custom_fusion.2, f32[384,1280]{0,1:T(8,128)} %copy.78), kind=kOutput, calls=%fused_computation.17 | convolution fusion | flops 1007616000 | bytes 8126464 | tf_op jit(solution)/shard_map/dot_general | solution.py:125
  139.3 6.1 %gather_fusion = f32[1024]{0:T(1024)S(1)} fusion(f32[32768]{0:T(1024)S(1)} %copy-done.1, s32[1024]{0:T(1024)S(1)} %fusion.41), kind=kCustom, calls=%fused_computation.6 | custom fusion | bytes 12288 | tf_op jit(solution)/shard_map/jit(_take)/gather | solution.py:70
  145.5 27.4 %reduce-scatter.3.cloned.1.call-done = f32[128,384]{0,1:T(8,128)} async-done(((f32[1024,384]{0,1:T(8,128)}), f32[128,384]{0,1:T(8,128)}) %reduce-scatter.3.cloned.1.call-update) | async-done | bytes 196624 | tf_op jit(solution)/shard_map/reduce_scatter | solution.py:124
  173.9 15.2 %all_gather.7 = bf16[384,1024]{1,0:T(8,128)(2,1)S(1)} all-gather(bf16[384,128]{1,0:T(8,128)(2,1)S(1)} %fusion.38), channel_id=1, replica_groups=mesh['lines'=4,'buses'=8] {'buses'}, dimensions={1}, use_global_device_ids=true | all-gather | bytes 884736 | tf_op jit(solution)/shard_map/all_gather | solution.py:89
  189.1 2.2 convolution_convert_fusion
  195.7 45.8 %all-reduce.5.cloned.1.call-done = bf16[384,1280]{1,0:T(8,128)(2,1)} async-done(((bf16[384,1280]{1,0:T(8,128)(2,1)}), bf16[384,1280]{1,0:T(8,128)(2,1)}) %all-reduce.5.cloned.1.call-update) | async-done | bytes 983056 | tf_op jit(solution)/shard_map/psum | solution.py:91
  241.5 2.5 copy.79
  244.0 2.8 gather_fusion.4
  247.7 4.6 %all-to-all-start.3 = ((bf16[384,8,32]{0,2,1:T(8,128)(2,1)}), bf16[384,8,32]{0,2,1:T(8,128)(2,1)}, u32[]{:S(2)}, u32[]{:S(2)}) async-start(bf16[384,8,32]{0,2,1:T(8,128)(2,1)} %bitcast.18), calls=%async_computation.4 | async-start | bytes 393216 | tf_op jit(solution)/shard_map/all_to_all | solution.py:93
  252.3 17.1 %psum.29 = f32[384]{0:T(512)S(1)} all-reduce(f32[384]{0:T(512)S(1)} %add_subtract_fusion.1), channel_id=1, replica_groups=mesh['lines'=4,'buses'=8] {'buses'}, use_global_device_ids=true, to_apply=%region_9.13 | all-reduce | flops 384 | bytes 3072 | tf_op jit(solution)/shard_map/psum | solution.py:132
  273.7 2.0 scatter_custom_fusion.3
  276.4 4.2 %all-to-all-start.4 = ((bf16[384,8,32]{0,2,1:T(8,128)(2,1)}), bf16[384,8,32]{0,2,1:T(8,128)(2,1)}, u32[]{:S(2)}, u32[]{:S(2)}) async-start(bf16[384,8,32]{0,2,1:T(8,128)(2,1)} %bitcast.135), calls=%async_computation.5 | async-start | bytes 393216 | tf_op jit(solution)/shard_map/all_to_all | solution.py:118
  283.3 2.5 gather_fusion.6
  286.6 2.0 fusion.50
  290.6 4.7 %scatter_custom_fusion.4 = f32[384,1280]{0,1:T(8,128)} fusion(s32[384]{0:T(512)} %add_reduce_fusion, f32[]{:T(128)} %constant.64.clone.1, f32[384,128]{0,1:T(8,128)S(1)} %copy.86, f32[]{:T(128)} %constant.140, f32[384,256]{0,1:T(8,128)} %bitcast_convert_fusion.2), kind=kCustom, calls=%fused_computation.20 | custom fusion | flops 294912 | bytes 2556928 | tf_op jit(solution)/shard_map/add | solution.py:122
  295.3 4.5 %convolution_bitcast_fusion = f32[1024,384]{0,1:T(8,128)} fusion(bf16[1024,1280]{1,0:T(8,128)(2,1)S(1)} %copy-done, f32[384,1280]{0,1:T(8,128)} %scatter_custom_fusion.4, f32[384,1280]{0,1:T(8,128)} %copy.78), kind=kOutput, calls=%fused_computation.16 | convolution fusion | flops 1007616000 | bytes 8126464 | tf_op jit(solution)/shard_map/dot_general | solution.py:125
  303.2 16.8 %psum.31 = f32[384]{0:T(512)S(1)} all-reduce(f32[384]{0:T(512)S(1)} %add_subtract_fusion), channel_id=1, replica_groups=mesh['lines'=4,'buses'=8] {'buses'}, use_global_device_ids=true, to_apply=%region_18.22 | all-reduce | flops 384 | bytes 3072 | tf_op jit(solution)/shard_map/psum | solution.py:132
  320.6 13.8 %reduce-scatter.5.cloned.1.call-done = f32[128,384]{0,1:T(8,128)} async-done(((f32[1024,384]{0,1:T(8,128)}), f32[128,384]{0,1:T(8,128)}) %reduce-scatter.5.cloned.1.call-update) | async-done | bytes 196624 | tf_op jit(solution)/shard_map/reduce_scatter | solution.py:124
  (166 shorter events, 43.4 us)
Async XLA Ops:
  7.2 26.3 %copy-start = (bf16[1024,1280]{1,0:T(8,128)(2,1)S(1)}, bf16[1024,1280]{1,0:T(8,128)(2,1)}, u32[]{:S(2)}) copy-start(bf16[1024,1280]{1,0:T(8,128)(2,1)} %param.23) | copy-start | bytes 7864324
  9.0 100.4 %copy-start.16 = (pred[256]{0:T(512)(128)(4,1)}, pred[256]{0:T(512)(128)(4,1)S(1)}, u32[]{:S(2)}) copy-start(pred[256]{0:T(512)(128)(4,1)S(1)} %get-tuple-element.33) | copy-start | bytes 772
  9.0 102.3 %copy-start.22 = (s32[256]{0:T(256)}, s32[256]{0:T(256)S(1)}, u32[]{:S(2)}) copy-start(s32[256]{0:T(256)S(1)} %get-tuple-element.34) | copy-start | bytes 3076
  11.1 25.9 %all-to-all-start = ((s32[1,8,32]{2,0,1:T(1,128)}), s32[1,8,32]{2,0,1:T(1,128)S(1)}, u32[]{:S(2)}, u32[]{:S(2)}) async-start(s32[1,8,32]{2,0,1:T(1,128)} %all_to_all.30), calls=%async_computation | async-start | bytes 8192 | tf_op jit(solution)/shard_map/all_to_all | solution.py:68
  17.4 70.2 %all-reduce.3.cloned.1.call-start = ((), (), s32[]{:S(2)}) async-start(), calls=%async_computation.7 | async-start | bytes 1966080 | tf_op jit(solution)/shard_map/psum | solution.py:91
  37.0 87.7 %copy-start.25 = (pred[128]{0:T(512)(128)(4,1)}, pred[128]{0:T(512)(128)(4,1)S(1)}, u32[]{:S(2)}) copy-start(pred[128]{0:T(512)(128)(4,1)S(1)} %get-tuple-element.35) | copy-start | bytes 388
  37.1 55.8 %copy-start.11 = (s32[1024]{0:T(1024)}, s32[1024]{0:T(1024)S(1)}, u32[]{:S(2)}) copy-start(s32[1024]{0:T(1024)S(1)} %pad_clamp_fusion.2) | copy-start | bytes 12292
  37.1 55.8 %copy-start.30 = (pred[256]{0:T(512)(128)(4,1)}, pred[256]{0:T(512)(128)(4,1)S(1)}, u32[]{:S(2)}) copy-start(pred[256]{0:T(512)(128)(4,1)S(1)} %compare_and_fusion.2) | copy-start | bytes 772
  90.2 8.1 %copy-start.40 = (f32[128]{0:T(128)S(1)}, f32[128]{0:T(128)}, u32[]{:S(2)}) copy-start(f32[128]{0:T(128)} %param.33) | copy-start | bytes 1540
  90.2 9.3 %copy-start.23 = (f32[128]{0:T(128)S(1)}, f32[128]{0:T(128)}, u32[]{:S(2)}) copy-start(f32[128]{0:T(128)} %param.34) | copy-start | bytes 1540
  93.7 13.0 %all-to-all-start.1 = ((bf16[384,8,32]{0,2,1:T(8,128)(2,1)}), bf16[384,8,32]{0,2,1:T(8,128)(2,1)}, u32[]{:S(2)}, u32[]{:S(2)}) async-start(bf16[384,8,32]{0,2,1:T(8,128)(2,1)} %bitcast.4), calls=%async_computation.1 | async-start | bytes 393216 | tf_op jit(solution)/shard_map/all_to_all | solution.py:93
  98.3 26.4 %copy-start.27 = (f32[128]{0:T(128)}, f32[128]{0:T(128)S(1)}, u32[]{:S(2)}) copy-start(f32[128]{0:T(128)S(1)} %broadcast_multiply_fusion.2) | copy-start | bytes 1540
  103.7 5.7 %copy-start.12 = (s32[1024]{0:T(1024)}, s32[1024]{0:T(1024)S(1)}, u32[]{:S(2)}) copy-start(s32[1024]{0:T(1024)S(1)} %pad_clamp_fusion.1) | copy-start | bytes 12292
  103.7 5.7 %copy-start.9 = (f32[256]{0:T(256)}, f32[256]{0:T(256)S(1)}, u32[]{:S(2)}) copy-start(f32[256]{0:T(256)S(1)} %broadcast_multiply_fusion) | copy-start | bytes 3076
  111.3 11.7 %copy-start.2 = (f32[384,256]{0,1:T(8,128)}, f32[384,256]{0,1:T(8,128)S(1)}, u32[]{:S(2)}) copy-start(f32[384,256]{0,1:T(8,128)S(1)} %get-tuple-element.32) | copy-start | bytes 1179652
  115.1 12.3 %all-to-all-start.2 = ((bf16[384,8,32]{0,2,1:T(8,128)(2,1)}), bf16[384,8,32]{0,2,1:T(8,128)(2,1)}, u32[]{:S(2)}, u32[]{:S(2)}) async-start(bf16[384,8,32]{0,2,1:T(8,128)(2,1)} %bitcast.136), calls=%async_computation.2 | async-start | bytes 393216 | tf_op jit(solution)/shard_map/all_to_all | solution.py:118
  119.2 53.8 %reduce-scatter.3.cloned.1.call-start = ((), (), s32[]{:S(2)}) async-start(), calls=%async_computation.8 | async-start | bytes 1769472 | tf_op jit(solution)/shard_map/reduce_scatter | solution.py:124
  138.4 103.1 %all-reduce.5.cloned.1.call-start = ((), (), s32[]{:S(2)}) async-start(), calls=%async_computation.9 | async-start | bytes 1966080 | tf_op jit(solution)/shard_map/psum | solution.py:91
  139.3 33.7 %copy-start.3 = (f32[384,128]{1,0:T(8,128)S(1)}, f32[384,128]{1,0:T(8,128)}, u32[]{:S(2)}) copy-start(f32[384,128]{1,0:T(8,128)} %param.38) | copy-start | bytes 589828
  193.0 48.5 %copy-start.32 = (pred[384]{0:T(512)(128)(4,1)}, pred[384]{0:T(512)(128)(4,1)S(1)}, u32[]{:S(2)}) copy-start(pred[384]{0:T(512)(128)(4,1)S(1)} %fusion.42) | copy-start | bytes 1156
  193.1 48.5 %copy-start.34 = (f32[128]{0:T(128)}, f32[128]{0:T(128)S(1)}, u32[]{:S(2)}) copy-start(f32[128]{0:T(128)S(1)} %get-tuple-element.43) | copy-start | bytes 1540
  195.7 51.2 %copy-start.31 = (pred[256]{0:T(512)(128)(4,1)S(1)}, pred[256]{0:T(512)(128)(4,1)}, u32[]{:S(2)}) copy-start(pred[256]{0:T(512)(128)(4,1)} %copy-done.30) | copy-start | bytes 772
  244.0 8.2 %copy-start.13 = (f32[384]{0:T(512)S(1)}, f32[384]{0:T(512)}, u32[]{:S(2)}) copy-start(f32[384]{0:T(512)} %get-tuple-element.31) | copy-start | bytes 4612
  244.0 8.2 %copy-start.14 = (f32[384]{0:T(512)S(1)}, f32[384]{0:T(512)}, u32[]{:S(2)}) copy-start(f32[384]{0:T(512)} %get-tuple-element.28) | copy-start | bytes 4612
  247.7 21.8 %all-to-all-start.3 = ((bf16[384,8,32]{0,2,1:T(8,128)(2,1)}), bf16[384,8,32]{0,2,1:T(8,128)(2,1)}, u32[]{:S(2)}, u32[]{:S(2)}) async-start(bf16[384,8,32]{0,2,1:T(8,128)(2,1)} %bitcast.18), calls=%async_computation.4 | async-start | bytes 393216 | tf_op jit(solution)/shard_map/all_to_all | solution.py:93
  276.4 10.2 %copy-start.24 = (f32[128]{0:T(128)S(1)}, f32[128]{0:T(128)}, u32[]{:S(2)}) copy-start(f32[128]{0:T(128)} %param.34) | copy-start | bytes 1540
  276.4 10.2 %copy-start.26 = (pred[128]{0:T(512)(128)(4,1)S(1)}, pred[128]{0:T(512)(128)(4,1)}, u32[]{:S(2)}) copy-start(pred[128]{0:T(512)(128)(4,1)} %copy-done.25) | copy-start | bytes 388
  276.4 10.2 %copy-start.28 = (f32[128]{0:T(128)S(1)}, f32[128]{0:T(128)}, u32[]{:S(2)}) copy-start(f32[128]{0:T(128)} %copy-done.27) | copy-start | bytes 1540
  276.4 10.2 %copy-start.29 = (f32[128]{0:T(128)S(1)}, f32[128]{0:T(128)}, u32[]{:S(2)}) copy-start(f32[128]{0:T(128)} %neg.12) | copy-start | bytes 1540
  276.4 12.5 %all-to-all-start.4 = ((bf16[384,8,32]{0,2,1:T(8,128)(2,1)}), bf16[384,8,32]{0,2,1:T(8,128)(2,1)}, u32[]{:S(2)}, u32[]{:S(2)}) async-start(bf16[384,8,32]{0,2,1:T(8,128)(2,1)} %bitcast.135), calls=%async_computation.5 | async-start | bytes 393216 | tf_op jit(solution)/shard_map/all_to_all | solution.py:118
  280.6 53.8 %reduce-scatter.5.cloned.1.call-start = ((), (), s32[]{:S(2)}) async-start(), calls=%async_computation.10 | async-start | bytes 1769472 | tf_op jit(solution)/shard_map/reduce_scatter | solution.py:124
  299.8 34.6 %copy-start.4 = (f32[384,128]{1,0:T(8,128)S(1)}, f32[384,128]{1,0:T(8,128)}, u32[]{:S(2)}) copy-start(f32[384,128]{1,0:T(8,128)} %param.38) | copy-start | bytes 589828
  (19 other events, 52.2 us)
Sparse Core Ops, SparseCore 0:
  35.8 51.8 all-reduce.2
  138.5 34.3 reduce-scatter.2
  191.4 50.0 all-reduce.4
  300.0 34.3 reduce-scatter.4
where the time goes:
time: 344 us; the launch traced here: 343 us
  waiting for transfers between devices  141 us (41%)
  blocking collectives  64.1 us (19%)
  other arithmetic  44.4 us (13%)
  local copies, waits for them, and re-layouts  41.6 us (12%)
  starting transfers between devices  23.9 us (7%)
  between operations  14.3 us (4%)
  matrix products  13.4 us (4%)
    psum x2, waiting for transfers between devices, shards(): lax.psum(partial_value.astype(jnp.bfloat16), 'lines').astype(jnp.float32)  96.4 us
    reduce_scatter x2, waiting for transfers between devices, shards(): lax.psum_scatter(lax.dot_general(ptdf, inj_low, (((1,), (1,)), ((), ())),...  41.2 us
    psum x2, blocking collectives, shards(): balance = lax.psum(balance_term, 'buses')  34 us
    all_gather x2, blocking collectives, shards(): lax.all_gather(dual_flow.astype(jnp.bfloat16), 'buses', axis=1, tiled=True)  30.2 us
    add x2, other arithmetic, shards(): injection = empty.at[:, arrived_bus].add(received) + stor_inject - load  9.35 us
    all_to_all x2, starting transfers between devices, shards(): lax.all_to_all(jnp.take(bus_price, arrived_bus, axis=1).astype(jnp.bfloat...  9.21 us
    dot_general x2, matrix products, shards(): lax.dot_general(ptdf, inj_low, (((1,), (1,)), ((), ())), preferred_elemen...  9.06 us
    all_to_all x2, starting transfers between devices, shards(): lax.all_to_all(slotted.astype(jnp.bfloat16), 'buses', split_axis=1, conca...  8.18 us
  transfers between devices with their start and end apart: 9, of which 7 were waited for; matrix products, arithmetic and copies ran while one was open for 11% of the time, Pallas kernels for 0%

commit v1 on v0

--- a/solution.py
+++ b/solution.py
@@ -129,7 +129,11 @@
             scatter_dimension=0,
             tiled=True,
         ).T
-        balance = lax.psum(balance_term, "buses")
+        balance = balance_term
+        for hop in (1, 2, 4):
+            balance = balance + lax.ppermute(
+                balance, "buses", [(dev, dev ^ hop) for dev in range(8)]
+            )
         dual_flow = dual_step(dual_flow, flow_share, SIGMA_FLOW, -limit_share, limit_share)
         price_level = price_level + KAPPA / total_units * balance
         dual_store = dual_step(

time: 344 us -> 336 us (0.977)
  blocking collectives: 64.1 us -> 30.2 us
  waiting for transfers between devices: 141 us -> 159 us
  starting transfers between devices: 23.9 us -> 29.6 us
    psum x2 -> x0, blocking collectives: 34 us -> none  [shards(): balance = lax.psum(balance_term, 'buses')]
    reduce_scatter x2, waiting for transfers between devices: 41.2 us -> 51.5 us  [shards(): lax.psum_scatter(lax.dot_general(ptdf, inj_low, (((1,), (1,)), ((), ())),...]
    ppermute x0 -> x6, waiting for transfers between devices: none -> 5.93 us  [shards(): lax.ppermute(balance, 'buses', [(dev, dev ^ hop) for dev in range(8)])]
    all_to_all x2, waiting for transfers between devices: 2.96 us -> 8.79 us  [shards(): lax.all_to_all(jnp.take(bus_price, arrived_bus, axis=1).astype(jnp.bfloat...]
    ppermute x0 -> x6, starting transfers between devices: none -> 5.73 us  [shards(): lax.ppermute(balance, 'buses', [(dev, dev ^ hop) for dev in range(8)])]
    psum x2, waiting for transfers between devices: 96.4 us -> 92.8 us  [shards(): lax.psum(partial_value.astype(jnp.bfloat16), 'lines').astype(jnp.float32)]
    unnamed x87 -> x83, local copies, waits for them, and re-layouts: 7.12 us -> 6.62 us
  transfers between devices with their start and end apart: 9 -> 15, of which waited for: 7 -> 12; matrix products, arithmetic and copies ran while one was open for 11% -> 14% of each run, Pallas kernels for 0% -> 0%
where the time goes in v1:
time: 336 us; the launch traced here: 334 us
  waiting for transfers between devices  159 us (47%)
  other arithmetic  45.4 us (14%)
  local copies, waits for them, and re-layouts  41.8 us (12%)
  blocking collectives  30.2 us (9%)
  starting transfers between devices  29.6 us (9%)
  between operations  14.3 us (4%)
  matrix products  13.4 us (4%)
    psum x2, waiting for transfers between devices, shards(): lax.psum(partial_value.astype(jnp.bfloat16), 'lines').astype(jnp.float32)  92.8 us
    reduce_scatter x2, waiting for transfers between devices, shards(): lax.psum_scatter(lax.dot_general(ptdf, inj_low, (((1,), (1,)), ((), ())),...  51.5 us
    all_gather x2, blocking collectives, shards(): lax.all_gather(dual_flow.astype(jnp.bfloat16), 'buses', axis=1, tiled=True)  30.2 us
    add x2, other arithmetic, shards(): injection = empty.at[:, arrived_bus].add(received) + stor_inject - load  9.32 us
    all_to_all x2, starting transfers between devices, shards(): lax.all_to_all(jnp.take(bus_price, arrived_bus, axis=1).astype(jnp.bfloat...  9.21 us
    dot_general x2, matrix products, shards(): lax.dot_general(ptdf, inj_low, (((1,), (1,)), ((), ())), preferred_elemen...  9.1 us
    all_to_all x2, waiting for transfers between devices, shards(): lax.all_to_all(jnp.take(bus_price, arrived_bus, axis=1).astype(jnp.bfloat...  8.79 us
    all_to_all x2, starting transfers between devices, shards(): lax.all_to_all(slotted.astype(jnp.bfloat16), 'buses', split_axis=1, conca...  8.18 us
  transfers between devices with their start and end apart: 15, of which 12 were waited for; matrix products, arithmetic and copies ran while one was open for 14% of the time, Pallas kernels for 0%

profile of v1, /device:TPU:0, one launch (start us, length us, event | category | flops | bytes accessed | tf_op | source)
XLA Modules:
  0.0 334.2 jit_solution(662771394135945724)
XLA Ops:
  11.1 6.4 %all-to-all-start = ((s32[1,8,32]{2,0,1:T(1,128)}), s32[1,8,32]{2,0,1:T(1,128)S(1)}, u32[]{:S(2)}, u32[]{:S(2)}) async-start(s32[1,8,32]{2,0,1:T(1,128)} %all_to_all.30), calls=%async_computation | async-start | bytes 8192 | tf_op jit(solution)/shard_map/all_to_all | solution.py:68
  18.4 15.0 %all_gather.6 = bf16[384,1024]{1,0:T(8,128)(2,1)S(1)} all-gather(bf16[384,128]{1,0:T(8,128)(2,1)S(1)} %convert_element_type.65), channel_id=1, replica_groups=mesh['lines'=4,'buses'=8] {'buses'}, dimensions={1}, use_global_device_ids=true | all-gather | bytes 884736 | tf_op jit(solution)/shard_map/all_gather | solution.py:89
  33.4 2.2 convolution_convert_fusion.1
  37.1 50.5 %all-reduce.3.cloned.1.call-done = bf16[384,1280]{1,0:T(8,128)(2,1)} async-done(((bf16[384,1280]{1,0:T(8,128)(2,1)}), bf16[384,1280]{1,0:T(8,128)(2,1)}) %all-reduce.3.cloned.1.call-update) | async-done | bytes 983056 | tf_op jit(solution)/shard_map/psum | solution.py:91
  87.7 2.5 copy.69
  90.2 2.7 gather_fusion.1
  93.7 4.6 %all-to-all-start.1 = ((bf16[384,8,32]{0,2,1:T(8,128)(2,1)}), bf16[384,8,32]{0,2,1:T(8,128)(2,1)}, u32[]{:S(2)}, u32[]{:S(2)}) async-start(bf16[384,8,32]{0,2,1:T(8,128)(2,1)} %bitcast.4), calls=%async_computation.1 | async-start | bytes 393216 | tf_op jit(solution)/shard_map/all_to_all | solution.py:93
  100.8 2.9 copy.78
  103.8 2.9 all-to-all-done.1
  111.3 2.2 scatter_custom_fusion.1
  115.2 4.0 %all-to-all-start.2 = ((bf16[384,8,32]{0,2,1:T(8,128)(2,1)}), bf16[384,8,32]{0,2,1:T(8,128)(2,1)}, u32[]{:S(2)}, u32[]{:S(2)}) async-start(bf16[384,8,32]{0,2,1:T(8,128)(2,1)} %bitcast.136), calls=%async_computation.2 | async-start | bytes 393216 | tf_op jit(solution)/shard_map/all_to_all | solution.py:118
  119.9 3.1 gather_fusion.3
  124.7 2.5 fusion.53
  129.2 4.7 %scatter_custom_fusion.2 = f32[384,1280]{0,1:T(8,128)} fusion(s32[384]{0:T(512)} %add_reduce_fusion, f32[]{:T(128)} %constant.64.clone.1, f32[384,128]{0,1:T(8,128)S(1)} %copy.77, f32[]{:T(128)} %constant.140, f32[384,256]{0,1:T(8,128)} %bitcast_convert_fusion.4), kind=kCustom, calls=%fused_computation.22 | custom fusion | flops 294912 | bytes 2556928 | tf_op jit(solution)/shard_map/add | solution.py:122
  133.8 4.6 %convolution_bitcast_fusion.1 = f32[1024,384]{0,1:T(8,128)} fusion(bf16[1024,1280]{1,0:T(8,128)(2,1)S(1)} %copy-done, f32[384,1280]{0,1:T(8,128)} %scatter_custom_fusion.2, f32[384,1280]{0,1:T(8,128)} %copy.78), kind=kOutput, calls=%fused_computation.17 | convolution fusion | flops 1007616000 | bytes 8126464 | tf_op jit(solution)/shard_map/dot_general | solution.py:125
  139.3 6.1 %gather_fusion = f32[1024]{0:T(1024)S(1)} fusion(f32[32768]{0:T(1024)S(1)} %copy-done.1, s32[1024]{0:T(1024)S(1)} %fusion.41), kind=kCustom, calls=%fused_computation.6 | custom fusion | bytes 12288 | tf_op jit(solution)/shard_map/jit(_take)/gather | solution.py:70
  145.6 27.5 %reduce-scatter.3.cloned.1.call-done = f32[128,384]{0,1:T(8,128)} async-done(((f32[1024,384]{0,1:T(8,128)}), f32[128,384]{0,1:T(8,128)}) %reduce-scatter.3.cloned.1.call-update) | async-done | bytes 196624 | tf_op jit(solution)/shard_map/reduce_scatter | solution.py:124
  174.0 15.2 %all_gather.7 = bf16[384,1024]{1,0:T(8,128)(2,1)S(1)} all-gather(bf16[384,128]{1,0:T(8,128)(2,1)S(1)} %fusion.38), channel_id=1, replica_groups=mesh['lines'=4,'buses'=8] {'buses'}, dimensions={1}, use_global_device_ids=true | all-gather | bytes 884736 | tf_op jit(solution)/shard_map/all_gather | solution.py:89
  189.2 2.2 convolution_convert_fusion
  195.7 2.8 collective-permute-done.1
  199.4 42.3 %all-reduce.5.cloned.1.call-done = bf16[384,1280]{1,0:T(8,128)(2,1)} async-done(((bf16[384,1280]{1,0:T(8,128)(2,1)}), bf16[384,1280]{1,0:T(8,128)(2,1)}) %all-reduce.5.cloned.1.call-update) | async-done | bytes 983056 | tf_op jit(solution)/shard_map/psum | solution.py:91
  241.6 2.5 copy.79
  244.1 2.9 gather_fusion.4
  247.8 4.6 %all-to-all-start.3 = ((bf16[384,8,32]{0,2,1:T(8,128)(2,1)}), bf16[384,8,32]{0,2,1:T(8,128)(2,1)}, u32[]{:S(2)}, u32[]{:S(2)}) async-start(bf16[384,8,32]{0,2,1:T(8,128)(2,1)} %bitcast.18), calls=%async_computation.4 | async-start | bytes 393216 | tf_op jit(solution)/shard_map/all_to_all | solution.py:93
  255.0 5.8 %all-to-all-done.3 = bf16[384,8,32]{0,2,1:T(8,128)(2,1)} async-done(((bf16[384,8,32]{0,2,1:T(8,128)(2,1)}), bf16[384,8,32]{0,2,1:T(8,128)(2,1)}, u32[]{:S(2)}, u32[]{:S(2)}) %all-to-all-start.3) | async-done | bytes 196640 | tf_op jit(solution)/shard_map/all_to_all | solution.py:93
  265.0 2.0 scatter_custom_fusion.3
  267.8 4.2 %all-to-all-start.4 = ((bf16[384,8,32]{0,2,1:T(8,128)(2,1)}), bf16[384,8,32]{0,2,1:T(8,128)(2,1)}, u32[]{:S(2)}, u32[]{:S(2)}) async-start(bf16[384,8,32]{0,2,1:T(8,128)(2,1)} %bitcast.135), calls=%async_computation.5 | async-start | bytes 393216 | tf_op jit(solution)/shard_map/all_to_all | solution.py:118
  274.6 2.5 gather_fusion.6
  281.9 4.7 %scatter_custom_fusion.4 = f32[384,1280]{0,1:T(8,128)} fusion(s32[384]{0:T(512)} %add_reduce_fusion, f32[]{:T(128)} %constant.64.clone.1, f32[384,128]{0,1:T(8,128)S(1)} %copy.86, f32[]{:T(128)} %constant.140, f32[384,256]{0,1:T(8,128)} %bitcast_convert_fusion.2), kind=kCustom, calls=%fused_computation.20 | custom fusion | flops 294912 | bytes 2556928 | tf_op jit(solution)/shard_map/add | solution.py:122
  286.6 4.5 %convolution_bitcast_fusion = f32[1024,384]{0,1:T(8,128)} fusion(bf16[1024,1280]{1,0:T(8,128)(2,1)S(1)} %copy-done, f32[384,1280]{0,1:T(8,128)} %scatter_custom_fusion.4, f32[384,1280]{0,1:T(8,128)} %copy.78), kind=kOutput, calls=%fused_computation.16 | convolution fusion | flops 1007616000 | bytes 8126464 | tf_op jit(solution)/shard_map/dot_general | solution.py:125
  296.0 2.6 collective-permute-start.5
  301.8 24.0 %reduce-scatter.5.cloned.1.call-done = f32[128,384]{0,1:T(8,128)} async-done(((f32[1024,384]{0,1:T(8,128)}), f32[128,384]{0,1:T(8,128)}) %reduce-scatter.5.cloned.1.call-update) | async-done | bytes 196624 | tf_op jit(solution)/shard_map/reduce_scatter | solution.py:124
  (176 shorter events, 52.8 us)
Async XLA Ops:
  7.2 26.3 %copy-start = (bf16[1024,1280]{1,0:T(8,128)(2,1)S(1)}, bf16[1024,1280]{1,0:T(8,128)(2,1)}, u32[]{:S(2)}) copy-start(bf16[1024,1280]{1,0:T(8,128)(2,1)} %param.23) | copy-start | bytes 7864324
  9.0 100.4 %copy-start.17 = (pred[256]{0:T(512)(128)(4,1)}, pred[256]{0:T(512)(128)(4,1)S(1)}, u32[]{:S(2)}) copy-start(pred[256]{0:T(512)(128)(4,1)S(1)} %get-tuple-element.33) | copy-start | bytes 772
  9.0 102.3 %copy-start.23 = (s32[256]{0:T(256)}, s32[256]{0:T(256)S(1)}, u32[]{:S(2)}) copy-start(s32[256]{0:T(256)S(1)} %get-tuple-element.34) | copy-start | bytes 3076
  11.1 25.9 %all-to-all-start = ((s32[1,8,32]{2,0,1:T(1,128)}), s32[1,8,32]{2,0,1:T(1,128)S(1)}, u32[]{:S(2)}, u32[]{:S(2)}) async-start(s32[1,8,32]{2,0,1:T(1,128)} %all_to_all.30), calls=%async_computation | async-start | bytes 8192 | tf_op jit(solution)/shard_map/all_to_all | solution.py:68
  17.4 70.2 %all-reduce.3.cloned.1.call-start = ((), (), s32[]{:S(2)}) async-start(), calls=%async_computation.7 | async-start | bytes 1966080 | tf_op jit(solution)/shard_map/psum | solution.py:91
  37.0 87.7 %copy-start.26 = (pred[128]{0:T(512)(128)(4,1)}, pred[128]{0:T(512)(128)(4,1)S(1)}, u32[]{:S(2)}) copy-start(pred[128]{0:T(512)(128)(4,1)S(1)} %get-tuple-element.35) | copy-start | bytes 388
  37.1 55.8 %copy-start.12 = (s32[1024]{0:T(1024)}, s32[1024]{0:T(1024)S(1)}, u32[]{:S(2)}) copy-start(s32[1024]{0:T(1024)S(1)} %pad_clamp_fusion.2) | copy-start | bytes 12292
  37.1 55.8 %copy-start.31 = (pred[256]{0:T(512)(128)(4,1)}, pred[256]{0:T(512)(128)(4,1)S(1)}, u32[]{:S(2)}) copy-start(pred[256]{0:T(512)(128)(4,1)S(1)} %compare_and_fusion.2) | copy-start | bytes 772
  90.2 9.3 %copy-start.24 = (f32[128]{0:T(128)S(1)}, f32[128]{0:T(128)}, u32[]{:S(2)}) copy-start(f32[128]{0:T(128)} %param.34) | copy-start | bytes 1540
  93.7 13.0 %all-to-all-start.1 = ((bf16[384,8,32]{0,2,1:T(8,128)(2,1)}), bf16[384,8,32]{0,2,1:T(8,128)(2,1)}, u32[]{:S(2)}, u32[]{:S(2)}) async-start(bf16[384,8,32]{0,2,1:T(8,128)(2,1)} %bitcast.4), calls=%async_computation.1 | async-start | bytes 393216 | tf_op jit(solution)/shard_map/all_to_all | solution.py:93
  98.3 26.4 %copy-start.28 = (f32[128]{0:T(128)}, f32[128]{0:T(128)S(1)}, u32[]{:S(2)}) copy-start(f32[128]{0:T(128)S(1)} %broadcast_multiply_fusion.2) | copy-start | bytes 1540
  111.3 11.7 %copy-start.2 = (f32[384,256]{0,1:T(8,128)}, f32[384,256]{0,1:T(8,128)S(1)}, u32[]{:S(2)}) copy-start(f32[384,256]{0,1:T(8,128)S(1)} %get-tuple-element.32) | copy-start | bytes 1179652
  115.2 12.3 %all-to-all-start.2 = ((bf16[384,8,32]{0,2,1:T(8,128)(2,1)}), bf16[384,8,32]{0,2,1:T(8,128)(2,1)}, u32[]{:S(2)}, u32[]{:S(2)}) async-start(bf16[384,8,32]{0,2,1:T(8,128)(2,1)} %bitcast.136), calls=%async_computation.2 | async-start | bytes 393216 | tf_op jit(solution)/shard_map/all_to_all | solution.py:118
  119.2 53.9 %reduce-scatter.3.cloned.1.call-start = ((), (), s32[]{:S(2)}) async-start(), calls=%async_computation.8 | async-start | bytes 1769472 | tf_op jit(solution)/shard_map/reduce_scatter | solution.py:124
  138.4 103.2 %all-reduce.5.cloned.1.call-start = ((), (), s32[]{:S(2)}) async-start(), calls=%async_computation.9 | async-start | bytes 1966080 | tf_op jit(solution)/shard_map/psum | solution.py:91
  139.3 33.7 %copy-start.3 = (f32[384,128]{1,0:T(8,128)S(1)}, f32[384,128]{1,0:T(8,128)}, u32[]{:S(2)}) copy-start(f32[384,128]{1,0:T(8,128)} %param.38) | copy-start | bytes 589828
  193.7 1.2 collective-permute-start
  194.9 3.6 %collective-permute-start.1 = (f32[384]{0:T(512)S(1)}, f32[384]{0:T(512)S(1)}, u32[]{:S(2)}, u32[]{:S(2)}) collective-permute-start(f32[384]{0:T(512)S(1)} %add.218), channel_id=1, source_target_pairs={{0,2},{1,3},{2,0},{3,1},{4,6},{5,7},{6,4},{7,5},{8,10},{9,11},{10,... | collective-permute-start | bytes 4616 | tf_op jit(solution)/shard_map/ppermute | solution.py:134
  198.5 48.5 %copy-start.32 = (pred[256]{0:T(512)(128)(4,1)S(1)}, pred[256]{0:T(512)(128)(4,1)}, u32[]{:S(2)}) copy-start(pred[256]{0:T(512)(128)(4,1)} %copy-done.31) | copy-start | bytes 772
  198.5 56.4 %collective-permute-start.2 = (f32[384]{0:T(512)S(1)}, f32[384]{0:T(512)S(1)}, u32[]{:S(2)}, u32[]{:S(2)}) collective-permute-start(f32[384]{0:T(512)S(1)} %add.219), channel_id=1, source_target_pairs={{0,4},{1,5},{2,6},{3,7},{4,0},{5,1},{6,2},{7,3},{8,12},{9,13},{10,... | collective-permute-start | bytes 4616 | tf_op jit(solution)/shard_map/ppermute | solution.py:134
  247.8 13.0 %all-to-all-start.3 = ((bf16[384,8,32]{0,2,1:T(8,128)(2,1)}), bf16[384,8,32]{0,2,1:T(8,128)(2,1)}, u32[]{:S(2)}, u32[]{:S(2)}) async-start(bf16[384,8,32]{0,2,1:T(8,128)(2,1)} %bitcast.18), calls=%async_computation.4 | async-start | bytes 393216 | tf_op jit(solution)/shard_map/all_to_all | solution.py:93
  254.9 8.7 %copy-start.11 = (f32[256]{0:T(256)S(1)}, f32[256]{0:T(256)}, u32[]{:S(2)}) copy-start(f32[256]{0:T(256)} %copy-done.10) | copy-start | bytes 3076
  267.7 10.2 %copy-start.25 = (f32[128]{0:T(128)S(1)}, f32[128]{0:T(128)}, u32[]{:S(2)}) copy-start(f32[128]{0:T(128)} %param.34) | copy-start | bytes 1540
  267.7 10.2 %copy-start.27 = (pred[128]{0:T(512)(128)(4,1)S(1)}, pred[128]{0:T(512)(128)(4,1)}, u32[]{:S(2)}) copy-start(pred[128]{0:T(512)(128)(4,1)} %copy-done.26) | copy-start | bytes 388
  267.7 10.2 %copy-start.29 = (f32[128]{0:T(128)S(1)}, f32[128]{0:T(128)}, u32[]{:S(2)}) copy-start(f32[128]{0:T(128)} %copy-done.28) | copy-start | bytes 1540
  267.8 10.2 %copy-start.30 = (f32[128]{0:T(128)S(1)}, f32[128]{0:T(128)}, u32[]{:S(2)}) copy-start(f32[128]{0:T(128)} %neg.12) | copy-start | bytes 1540
  267.8 12.5 %all-to-all-start.4 = ((bf16[384,8,32]{0,2,1:T(8,128)(2,1)}), bf16[384,8,32]{0,2,1:T(8,128)(2,1)}, u32[]{:S(2)}, u32[]{:S(2)}) async-start(bf16[384,8,32]{0,2,1:T(8,128)(2,1)} %bitcast.135), calls=%async_computation.5 | async-start | bytes 393216 | tf_op jit(solution)/shard_map/all_to_all | solution.py:118
  271.9 53.9 %reduce-scatter.5.cloned.1.call-start = ((), (), s32[]{:S(2)}) async-start(), calls=%async_computation.10 | async-start | bytes 1769472 | tf_op jit(solution)/shard_map/reduce_scatter | solution.py:124
  291.1 34.7 %copy-start.4 = (f32[384,128]{1,0:T(8,128)S(1)}, f32[384,128]{1,0:T(8,128)}, u32[]{:S(2)}) copy-start(f32[384,128]{1,0:T(8,128)} %param.38) | copy-start | bytes 589828
  291.2 1.2 collective-permute-start.3
  292.4 3.6 %collective-permute-start.4 = (f32[384]{0:T(512)S(1)}, f32[384]{0:T(512)S(1)}, u32[]{:S(2)}, u32[]{:S(2)}) collective-permute-start(f32[384]{0:T(512)S(1)} %add.239), channel_id=1, source_target_pairs={{0,2},{1,3},{2,0},{3,1},{4,6},{5,7},{6,4},{7,5},{8,10},{9,11},{10,... | collective-permute-start | bytes 4616 | tf_op jit(solution)/shard_map/ppermute | solution.py:134
  296.0 5.2 %collective-permute-start.5 = (f32[384]{0:T(512)S(1)}, f32[384]{0:T(512)S(1)}, u32[]{:S(2)}, u32[]{:S(2)}) collective-permute-start(f32[384]{0:T(512)S(1)} %add.240), channel_id=1, source_target_pairs={{0,4},{1,5},{2,6},{3,7},{4,0},{5,1},{6,2},{7,3},{8,12},{9,13},{10,... | collective-permute-start | bytes 4616 | tf_op jit(solution)/shard_map/ppermute | solution.py:134
  (23 other events, 120.3 us)
Sparse Core Ops, SparseCore 0:
  35.8 51.8 all-reduce.2
  138.5 34.4 reduce-scatter.2
  191.5 50.0 all-reduce.4
  291.3 34.4 reduce-scatter.4
